TPU v7x, 512 devices: a whole 4x8x8 slice. The times are simulated.
512 devices in a mesh: blk: 32 (over x_hi, z, core), split: 16 (over x_lo, y).
Axes of the slice: x: 4 (x_hi: 2, x_lo: 2; x = x_hi * 2 + x_lo), y: 8, z: 8, core: 2. Of those that a mesh axis runs over, the one named last changes fastest.
Arguments:
- orbitals: float32 [16384, 512], P('blk'), may hold values from -6 to 6
- kernel: float32 [16384, 16, 1024], P('blk', 'split'), as said below
Outputs:
- exchange_out: float32 [16384, 512], P(('blk', 'split'))
Inputs may be any that keep to these rules, and one draw needn't show every extreme that they name: Z built from kernel as in the first step is a symmetric matrix.
All inputs are finite; a program needn't handle non-finite values.
Results may differ from a plain program's by a relative error of at most 0.00013.
Values sent between devices are 32-bit elements; how exact they have to be, the bound alone decides.
A program may use at most 64 MiB of HBM per device.

v0:
```python
import jax
import jax.numpy as jnp
from jax import lax
from jax.sharding import PartitionSpec as P


def shifted(value, axis, by):
    peers = lax.axis_size(axis)
    return lax.ppermute(value, axis, [(i, (i + by) % peers) for i in range(peers)])


def gram_weighted(orbitals, visitor, kernel, source):
    width = visitor.shape[0]
    kernel_tile = lax.dynamic_slice_in_dim(kernel, source * width, width, 1)
    correlation = lax.dot_general(
        orbitals,
        visitor,
        (((1,), (1,)), ((), ())),
        precision=lax.Precision.HIGHEST,
        preferred_element_type=jnp.float32,
    )
    return kernel_tile * correlation


def apply_rows(weights, visitor):
    return jnp.dot(
        weights, visitor, precision=lax.Precision.HIGHEST, preferred_element_type=jnp.float32
    )


def apply_back(weights, orbitals):
    return lax.dot_general(
        weights,
        orbitals,
        (((0,), (0,)), ((), ())),
        precision=lax.Precision.HIGHEST,
        preferred_element_type=jnp.float32,
    )


def move_pair(stacked):
    return shifted(stacked, "blk", 1)


def per_device(orbitals, kernel):
    nblocks = lax.axis_size("blk")
    nshares = lax.axis_size("split")
    block_id = lax.axis_index("blk")
    share_id = lax.axis_index("split")
    home_rows = orbitals.shape[0]
    share_rows = home_rows // nshares
    halfway = nblocks // 2
    kernel = kernel[:, 0, :]
    own = lax.dynamic_slice_in_dim(orbitals, share_id * share_rows, share_rows, 0)
    home = apply_rows(gram_weighted(orbitals, own, kernel, block_id), own)

    def advance(offset, state_now):
        stacked, partial_value = state_now
        stacked = move_pair(stacked)
        source = (block_id - offset) % nblocks
        weights = gram_weighted(orbitals, stacked[0], kernel, source)
        partial_value = partial_value + apply_rows(weights, stacked[0])
        carried = stacked[1] + apply_back(weights, orbitals)
        return (jnp.stack([stacked[0], carried]), partial_value)

    stacked = jnp.stack([own, jnp.zeros_like(own)])
    stacked, home = lax.fori_loop(1, halfway, advance, (stacked, home))
    back = shifted(stacked[1], "blk", -(halfway - 1))
    stacked = move_pair(stacked)
    source = (block_id - halfway) % nblocks
    home = home + apply_rows(gram_weighted(orbitals, stacked[0], kernel, source), stacked[0])
    folded = lax.psum_scatter(home, "split", scatter_dimension=0, tiled=True)
    return folded + back


def solution(mesh):
    placed = (P("blk", None), P("blk", "split", None))
    return jax.shard_map(
        per_device, mesh=mesh, in_specs=placed, out_specs=P(("blk", "split"), None), check_vma=False
    )
```

profile of v0, /device:TPU:4, one launch (start us, length us, event | category | flops | bytes accessed | tf_op | source)
XLA Modules:
  0.0 318.9 jit_solution(15741320878777375190)
XLA Ops:
  6.5 6.1 %copy.3 = f32[512,1,1024]{0,2,1:T(8,128)} copy(f32[512,1,1024]{2,1,0:T(1,128)} %param.5) | data formatting | bytes 4194304 | tf_op args[1]
  12.7 2.2 constant_dynamic-slice_fusion
  16.8 209.6 %while.17 = (s32[]{:T(128)}, f32[2,32,512]{2,1,0:T(8,128)S(1)}, f32[512,512]{1,0:T(8,128)S(1)}, s32[]{:T(128)}, f32[512,1024]{0,1:T(8,128)}, /*index=5*/f32[512,...) while((s32[]{:T(128)}, f32[2,32,512]{2,1,0:T(8,128)S(1)}, ...), condition=%wide.region_1.2_spmd, body=%wide.region_0.1_spmd.sunk | while | flops 302317568 | bytes 5636416 | solution.py:67
  16.8 1.9 collective-permute-start
  18.8 11.0 %collective-permute-done = f32[2,32,512]{2,1,0:T(8,128)S(1)} collective-permute-done((f32[2,32,512]{2,1,0:T(8,128)S(1)}, f32[2,32,512]{2,1,0:T(8,128)S(1)}, u32[]{:S(2)}, u32[]{:S(2)}) %collective-permute-start) | collective-permute-done | bytes 131104 | tf_op jit(solution)/shard_map/while/body/eval_jaxpr/ppermute | solution.py:9
  33.7 1.9 collective-permute-start
  35.6 7.9 %collective-permute-done = f32[2,32,512]{2,1,0:T(8,128)S(1)} collective-permute-done((f32[2,32,512]{2,1,0:T(8,128)S(1)}, f32[2,32,512]{2,1,0:T(8,128)S(1)}, u32[]{:S(2)}, u32[]{:S(2)}) %collective-permute-start) | collective-permute-done | bytes 131104 | tf_op jit(solution)/shard_map/while/body/eval_jaxpr/ppermute | solution.py:9
  47.5 1.9 collective-permute-start
  49.4 7.9 %collective-permute-done = f32[2,32,512]{2,1,0:T(8,128)S(1)} collective-permute-done((f32[2,32,512]{2,1,0:T(8,128)S(1)}, f32[2,32,512]{2,1,0:T(8,128)S(1)}, u32[]{:S(2)}, u32[]{:S(2)}) %collective-permute-start) | collective-permute-done | bytes 131104 | tf_op jit(solution)/shard_map/while/body/eval_jaxpr/ppermute | solution.py:9
  61.2 1.9 collective-permute-start
  63.2 7.9 %collective-permute-done = f32[2,32,512]{2,1,0:T(8,128)S(1)} collective-permute-done((f32[2,32,512]{2,1,0:T(8,128)S(1)}, f32[2,32,512]{2,1,0:T(8,128)S(1)}, u32[]{:S(2)}, u32[]{:S(2)}) %collective-permute-start) | collective-permute-done | bytes 131104 | tf_op jit(solution)/shard_map/while/body/eval_jaxpr/ppermute | solution.py:9
  76.9 7.9 %collective-permute-done = f32[2,32,512]{2,1,0:T(8,128)S(1)} collective-permute-done((f32[2,32,512]{2,1,0:T(8,128)S(1)}, f32[2,32,512]{2,1,0:T(8,128)S(1)}, u32[]{:S(2)}, u32[]{:S(2)}) %collective-permute-start) | collective-permute-done | bytes 131104 | tf_op jit(solution)/shard_map/while/body/eval_jaxpr/ppermute | solution.py:9
  90.7 7.9 %collective-permute-done = f32[2,32,512]{2,1,0:T(8,128)S(1)} collective-permute-done((f32[2,32,512]{2,1,0:T(8,128)S(1)}, f32[2,32,512]{2,1,0:T(8,128)S(1)}, u32[]{:S(2)}, u32[]{:S(2)}) %collective-permute-start) | collective-permute-done | bytes 131104 | tf_op jit(solution)/shard_map/while/body/eval_jaxpr/ppermute | solution.py:9
  102.5 1.9 collective-permute-start
  104.5 7.9 %collective-permute-done = f32[2,32,512]{2,1,0:T(8,128)S(1)} collective-permute-done((f32[2,32,512]{2,1,0:T(8,128)S(1)}, f32[2,32,512]{2,1,0:T(8,128)S(1)}, u32[]{:S(2)}, u32[]{:S(2)}) %collective-permute-start) | collective-permute-done | bytes 131104 | tf_op jit(solution)/shard_map/while/body/eval_jaxpr/ppermute | solution.py:9
  116.3 1.9 collective-permute-start
  118.2 7.9 %collective-permute-done = f32[2,32,512]{2,1,0:T(8,128)S(1)} collective-permute-done((f32[2,32,512]{2,1,0:T(8,128)S(1)}, f32[2,32,512]{2,1,0:T(8,128)S(1)}, u32[]{:S(2)}, u32[]{:S(2)}) %collective-permute-start) | collective-permute-done | bytes 131104 | tf_op jit(solution)/shard_map/while/body/eval_jaxpr/ppermute | solution.py:9
  130.1 1.9 collective-permute-start
  132.0 7.9 %collective-permute-done = f32[2,32,512]{2,1,0:T(8,128)S(1)} collective-permute-done((f32[2,32,512]{2,1,0:T(8,128)S(1)}, f32[2,32,512]{2,1,0:T(8,128)S(1)}, u32[]{:S(2)}, u32[]{:S(2)}) %collective-permute-start) | collective-permute-done | bytes 131104 | tf_op jit(solution)/shard_map/while/body/eval_jaxpr/ppermute | solution.py:9
  143.8 1.9 collective-permute-start
  145.8 7.9 %collective-permute-done = f32[2,32,512]{2,1,0:T(8,128)S(1)} collective-permute-done((f32[2,32,512]{2,1,0:T(8,128)S(1)}, f32[2,32,512]{2,1,0:T(8,128)S(1)}, u32[]{:S(2)}, u32[]{:S(2)}) %collective-permute-start) | collective-permute-done | bytes 131104 | tf_op jit(solution)/shard_map/while/body/eval_jaxpr/ppermute | solution.py:9
  157.6 1.9 collective-permute-start
  159.6 7.9 %collective-permute-done = f32[2,32,512]{2,1,0:T(8,128)S(1)} collective-permute-done((f32[2,32,512]{2,1,0:T(8,128)S(1)}, f32[2,32,512]{2,1,0:T(8,128)S(1)}, u32[]{:S(2)}, u32[]{:S(2)}) %collective-permute-start) | collective-permute-done | bytes 131104 | tf_op jit(solution)/shard_map/while/body/eval_jaxpr/ppermute | solution.py:9
  171.4 1.9 collective-permute-start
  173.3 7.9 %collective-permute-done = f32[2,32,512]{2,1,0:T(8,128)S(1)} collective-permute-done((f32[2,32,512]{2,1,0:T(8,128)S(1)}, f32[2,32,512]{2,1,0:T(8,128)S(1)}, u32[]{:S(2)}, u32[]{:S(2)}) %collective-permute-start) | collective-permute-done | bytes 131104 | tf_op jit(solution)/shard_map/while/body/eval_jaxpr/ppermute | solution.py:9
  187.1 7.9 %collective-permute-done = f32[2,32,512]{2,1,0:T(8,128)S(1)} collective-permute-done((f32[2,32,512]{2,1,0:T(8,128)S(1)}, f32[2,32,512]{2,1,0:T(8,128)S(1)}, u32[]{:S(2)}, u32[]{:S(2)}) %collective-permute-start) | collective-permute-done | bytes 131104 | tf_op jit(solution)/shard_map/while/body/eval_jaxpr/ppermute | solution.py:9
  200.9 7.9 %collective-permute-done = f32[2,32,512]{2,1,0:T(8,128)S(1)} collective-permute-done((f32[2,32,512]{2,1,0:T(8,128)S(1)}, f32[2,32,512]{2,1,0:T(8,128)S(1)}, u32[]{:S(2)}, u32[]{:S(2)}) %collective-permute-start) | collective-permute-done | bytes 131104 | tf_op jit(solution)/shard_map/while/body/eval_jaxpr/ppermute | solution.py:9
  214.6 7.9 %collective-permute-done = f32[2,32,512]{2,1,0:T(8,128)S(1)} collective-permute-done((f32[2,32,512]{2,1,0:T(8,128)S(1)}, f32[2,32,512]{2,1,0:T(8,128)S(1)}, u32[]{:S(2)}, u32[]{:S(2)}) %collective-permute-start) | collective-permute-done | bytes 131104 | tf_op jit(solution)/shard_map/while/body/eval_jaxpr/ppermute | solution.py:9
  228.4 8.0 %collective-permute-done.1 = f32[2,32,512]{2,1,0:T(8,128)S(1)} collective-permute-done((f32[2,32,512]{2,1,0:T(8,128)S(1)}, f32[2,32,512]{2,1,0:T(8,128)S(1)}, u32[]{:S(2)}, u32[]{:S(2)}) %collective-permute-start.1) | collective-permute-done | bytes 131104 | tf_op jit(solution)/shard_map/ppermute | solution.py:9
  237.3 1.9 convolution_add_fusion.1
  241.2 4.9 %collective-permute-done.2 = f32[32,512]{1,0:T(8,128)S(1)} collective-permute-done((f32[32,512]{1,0:T(8,128)S(1)}, f32[32,512]{1,0:T(8,128)S(1)}, u32[]{:S(2)}, u32[]{:S(2)}) %collective-permute-start.2) | collective-permute-done | bytes 65568 | tf_op jit(solution)/shard_map/ppermute | solution.py:9
  246.1 64.5 %reduce-scatter.2.cloned.1.call-done = f32[32,512]{1,0:T(8,128)} async-done(((f32[512,512]{1,0:T(8,128)}), f32[32,512]{1,0:T(8,128)}) %reduce-scatter.2.cloned.1.call-update) | async-done | bytes 65552 | tf_op jit(solution)/shard_map/reduce_scatter | solution.py:72
  (93 shorter events, 75.2 us)
Async XLA Ops:
  6.5 304.0 %reduce-scatter.2.cloned.1.call-start = ((), (), s32[]{:S(2)}) async-start(), calls=%async_computation.1 | async-start | bytes 1114112 | tf_op jit(solution)/shard_map/reduce_scatter | solution.py:72
  6.5 8.3 %copy-start = (f32[512,512]{1,0:T(8,128)S(1)}, f32[512,512]{1,0:T(8,128)}, u32[]{:S(2)}) copy-start(f32[512,512]{1,0:T(8,128)} %param.4) | copy-start | bytes 3145732
  16.8 13.0 %collective-permute-start = (f32[2,32,512]{2,1,0:T(8,128)S(1)}, f32[2,32,512]{2,1,0:T(8,128)S(1)}, u32[]{:S(2)}, u32[]{:S(2)}) collective-permute-start(f32[2,32,512]{2,1,0:T(8,128)S(1)} %get-tuple-element.226), channel_id=1, source_target_pairs={{0,16},{16,32},{32,48},{48,64},{64,80},{80,96},{96,112},{112,128},... | collective-permute-start | bytes 393224 | tf_op jit(solution)/shard_map/while/body/eval_jaxpr/ppermute | solution.py:9
  33.7 9.9 %collective-permute-start = (f32[2,32,512]{2,1,0:T(8,128)S(1)}, f32[2,32,512]{2,1,0:T(8,128)S(1)}, u32[]{:S(2)}, u32[]{:S(2)}) collective-permute-start(f32[2,32,512]{2,1,0:T(8,128)S(1)} %get-tuple-element.226), channel_id=1, source_target_pairs={{0,16},{16,32},{32,48},{48,64},{64,80},{80,96},{96,112},{112,128},... | collective-permute-start | bytes 393224 | tf_op jit(solution)/shard_map/while/body/eval_jaxpr/ppermute | solution.py:9
  47.5 9.9 %collective-permute-start = (f32[2,32,512]{2,1,0:T(8,128)S(1)}, f32[2,32,512]{2,1,0:T(8,128)S(1)}, u32[]{:S(2)}, u32[]{:S(2)}) collective-permute-start(f32[2,32,512]{2,1,0:T(8,128)S(1)} %get-tuple-element.226), channel_id=1, source_target_pairs={{0,16},{16,32},{32,48},{48,64},{64,80},{80,96},{96,112},{112,128},... | collective-permute-start | bytes 393224 | tf_op jit(solution)/shard_map/while/body/eval_jaxpr/ppermute | solution.py:9
  61.2 9.9 %collective-permute-start = (f32[2,32,512]{2,1,0:T(8,128)S(1)}, f32[2,32,512]{2,1,0:T(8,128)S(1)}, u32[]{:S(2)}, u32[]{:S(2)}) collective-permute-start(f32[2,32,512]{2,1,0:T(8,128)S(1)} %get-tuple-element.226), channel_id=1, source_target_pairs={{0,16},{16,32},{32,48},{48,64},{64,80},{80,96},{96,112},{112,128},... | collective-permute-start | bytes 393224 | tf_op jit(solution)/shard_map/while/body/eval_jaxpr/ppermute | solution.py:9
  75.0 9.9 %collective-permute-start = (f32[2,32,512]{2,1,0:T(8,128)S(1)}, f32[2,32,512]{2,1,0:T(8,128)S(1)}, u32[]{:S(2)}, u32[]{:S(2)}) collective-permute-start(f32[2,32,512]{2,1,0:T(8,128)S(1)} %get-tuple-element.226), channel_id=1, source_target_pairs={{0,16},{16,32},{32,48},{48,64},{64,80},{80,96},{96,112},{112,128},... | collective-permute-start | bytes 393224 | tf_op jit(solution)/shard_map/while/body/eval_jaxpr/ppermute | solution.py:9
  88.8 9.9 %collective-permute-start = (f32[2,32,512]{2,1,0:T(8,128)S(1)}, f32[2,32,512]{2,1,0:T(8,128)S(1)}, u32[]{:S(2)}, u32[]{:S(2)}) collective-permute-start(f32[2,32,512]{2,1,0:T(8,128)S(1)} %get-tuple-element.226), channel_id=1, source_target_pairs={{0,16},{16,32},{32,48},{48,64},{64,80},{80,96},{96,112},{112,128},... | collective-permute-start | bytes 393224 | tf_op jit(solution)/shard_map/while/body/eval_jaxpr/ppermute | solution.py:9
  102.5 9.9 %collective-permute-start = (f32[2,32,512]{2,1,0:T(8,128)S(1)}, f32[2,32,512]{2,1,0:T(8,128)S(1)}, u32[]{:S(2)}, u32[]{:S(2)}) collective-permute-start(f32[2,32,512]{2,1,0:T(8,128)S(1)} %get-tuple-element.226), channel_id=1, source_target_pairs={{0,16},{16,32},{32,48},{48,64},{64,80},{80,96},{96,112},{112,128},... | collective-permute-start | bytes 393224 | tf_op jit(solution)/shard_map/while/body/eval_jaxpr/ppermute | solution.py:9
  116.3 9.9 %collective-permute-start = (f32[2,32,512]{2,1,0:T(8,128)S(1)}, f32[2,32,512]{2,1,0:T(8,128)S(1)}, u32[]{:S(2)}, u32[]{:S(2)}) collective-permute-start(f32[2,32,512]{2,1,0:T(8,128)S(1)} %get-tuple-element.226), channel_id=1, source_target_pairs={{0,16},{16,32},{32,48},{48,64},{64,80},{80,96},{96,112},{112,128},... | collective-permute-start | bytes 393224 | tf_op jit(solution)/shard_map/while/body/eval_jaxpr/ppermute | solution.py:9
  130.1 9.9 %collective-permute-start = (f32[2,32,512]{2,1,0:T(8,128)S(1)}, f32[2,32,512]{2,1,0:T(8,128)S(1)}, u32[]{:S(2)}, u32[]{:S(2)}) collective-permute-start(f32[2,32,512]{2,1,0:T(8,128)S(1)} %get-tuple-element.226), channel_id=1, source_target_pairs={{0,16},{16,32},{32,48},{48,64},{64,80},{80,96},{96,112},{112,128},... | collective-permute-start | bytes 393224 | tf_op jit(solution)/shard_map/while/body/eval_jaxpr/ppermute | solution.py:9
  143.8 9.9 %collective-permute-start = (f32[2,32,512]{2,1,0:T(8,128)S(1)}, f32[2,32,512]{2,1,0:T(8,128)S(1)}, u32[]{:S(2)}, u32[]{:S(2)}) collective-permute-start(f32[2,32,512]{2,1,0:T(8,128)S(1)} %get-tuple-element.226), channel_id=1, source_target_pairs={{0,16},{16,32},{32,48},{48,64},{64,80},{80,96},{96,112},{112,128},... | collective-permute-start | bytes 393224 | tf_op jit(solution)/shard_map/while/body/eval_jaxpr/ppermute | solution.py:9
  157.6 9.9 %collective-permute-start = (f32[2,32,512]{2,1,0:T(8,128)S(1)}, f32[2,32,512]{2,1,0:T(8,128)S(1)}, u32[]{:S(2)}, u32[]{:S(2)}) collective-permute-start(f32[2,32,512]{2,1,0:T(8,128)S(1)} %get-tuple-element.226), channel_id=1, source_target_pairs={{0,16},{16,32},{32,48},{48,64},{64,80},{80,96},{96,112},{112,128},... | collective-permute-start | bytes 393224 | tf_op jit(solution)/shard_map/while/body/eval_jaxpr/ppermute | solution.py:9
  171.4 9.9 %collective-permute-start = (f32[2,32,512]{2,1,0:T(8,128)S(1)}, f32[2,32,512]{2,1,0:T(8,128)S(1)}, u32[]{:S(2)}, u32[]{:S(2)}) collective-permute-start(f32[2,32,512]{2,1,0:T(8,128)S(1)} %get-tuple-element.226), channel_id=1, source_target_pairs={{0,16},{16,32},{32,48},{48,64},{64,80},{80,96},{96,112},{112,128},... | collective-permute-start | bytes 393224 | tf_op jit(solution)/shard_map/while/body/eval_jaxpr/ppermute | solution.py:9
  185.1 9.9 %collective-permute-start = (f32[2,32,512]{2,1,0:T(8,128)S(1)}, f32[2,32,512]{2,1,0:T(8,128)S(1)}, u32[]{:S(2)}, u32[]{:S(2)}) collective-permute-start(f32[2,32,512]{2,1,0:T(8,128)S(1)} %get-tuple-element.226), channel_id=1, source_target_pairs={{0,16},{16,32},{32,48},{48,64},{64,80},{80,96},{96,112},{112,128},... | collective-permute-start | bytes 393224 | tf_op jit(solution)/shard_map/while/body/eval_jaxpr/ppermute | solution.py:9
  198.9 9.9 %collective-permute-start = (f32[2,32,512]{2,1,0:T(8,128)S(1)}, f32[2,32,512]{2,1,0:T(8,128)S(1)}, u32[]{:S(2)}, u32[]{:S(2)}) collective-permute-start(f32[2,32,512]{2,1,0:T(8,128)S(1)} %get-tuple-element.226), channel_id=1, source_target_pairs={{0,16},{16,32},{32,48},{48,64},{64,80},{80,96},{96,112},{112,128},... | collective-permute-start | bytes 393224 | tf_op jit(solution)/shard_map/while/body/eval_jaxpr/ppermute | solution.py:9
  212.7 9.9 %collective-permute-start = (f32[2,32,512]{2,1,0:T(8,128)S(1)}, f32[2,32,512]{2,1,0:T(8,128)S(1)}, u32[]{:S(2)}, u32[]{:S(2)}) collective-permute-start(f32[2,32,512]{2,1,0:T(8,128)S(1)} %get-tuple-element.226), channel_id=1, source_target_pairs={{0,16},{16,32},{32,48},{48,64},{64,80},{80,96},{96,112},{112,128},... | collective-permute-start | bytes 393224 | tf_op jit(solution)/shard_map/while/body/eval_jaxpr/ppermute | solution.py:9
  226.4 9.9 %collective-permute-start.1 = (f32[2,32,512]{2,1,0:T(8,128)S(1)}, f32[2,32,512]{2,1,0:T(8,128)S(1)}, u32[]{:S(2)}, u32[]{:S(2)}) collective-permute-start(f32[2,32,512]{2,1,0:T(8,128)S(1)} %get-tuple-element.162), channel_id=1, source_target_pairs={{0,16},{16,32},{32,48},{48,64},{64,80},{80,96},{96,112},{112,128},... | collective-permute-start | bytes 393224 | tf_op jit(solution)/shard_map/ppermute | solution.py:9
  239.3 6.8 %collective-permute-start.2 = (f32[32,512]{1,0:T(8,128)S(1)}, f32[32,512]{1,0:T(8,128)S(1)}, u32[]{:S(2)}, u32[]{:S(2)}) collective-permute-start(f32[32,512]{1,0:T(8,128)S(1)} %slice_bitcast_fusion.2), channel_id=1, source_target_pairs={{0,272},{16,288},{32,304},{48,320},{64,336},{80,352},{96,368},{112... | collective-permute-start | bytes 196616 | tf_op jit(solution)/shard_map/ppermute | solution.py:9
Sparse Core Ops, SparseCore 0:
  239.4 71.1 reduce-scatter.1
where the time goes:
time: 320 us; the launch traced here: 319 us
  waiting for transfers between devices  200 us (62%)
  matrix products  62 us (19%)
  starting transfers between devices  32.7 us (10%)
  between operations  13.5 us (4%)
  local copies, waits for them, and re-layouts  8.4 us (3%)
    ppermute x17, waiting for transfers between devices, shifted(): lax.ppermute(value, axis, [(i, (i + by) % peers) for i in range(peers)])  135 us
    reduce_scatter x1, waiting for transfers between devices, per_device(): folded = lax.psum_scatter(home, 'split', scatter_dimension=0, tiled=True)  64.5 us
    ppermute x17, starting transfers between devices, shifted(): lax.ppermute(value, axis, [(i, (i + by) % peers) for i in range(peers)])  32.6 us
    dot_general x17, matrix products, gram_weighted(): lax.dot_general(orbitals, visitor, (((1,), (1,)), ((), ())), precision=la...  30.5 us
    dot_general x17, matrix products, apply_rows(): jnp.dot(weights, visitor, precision=lax.Precision.HIGHEST, preferred_elem...  20.8 us
    dot_general x15, matrix products, apply_back(): lax.dot_general(weights, orbitals, (((0,), (0,)), ((), ())), precision=la...  10.6 us
  transfers between devices with their start and end apart: 18, of which 18 were waited for; matrix products, arithmetic and copies ran while one was open for 0% of the time, Pallas kernels for 0%

commit v1 on v0

v1 whole, which is shorter than its diff:
```python
import functools

import jax
import jax.numpy as jnp
from jax import lax
from jax.experimental import pallas as pl
from jax.experimental.pallas import tpu as pltpu
from jax.sharding import PartitionSpec as P

MESH = pl.DeviceIdType.MESH
F32 = jnp.float32
BF16 = jnp.bfloat16

NX, NZ, NC = 2, 8, 2
NXL, NY = 2, 8
SH = 32
NORB = 512
PB = 512

GATHER = [("gx",)] + [
    ("gz", plane, sign, hop)
    for plane in (0, 1)
    for sign in (1, -1)
    for hop in range(1, 5)
    if hop < 4 or sign == (1 if plane == 0 else -1)
]
CORE = [("gc", plane, off) for plane in (0, 1) for off in range(NZ)]
REDUCE = [
    ("r", plane, sign, dist)
    for plane in (0, 1)
    for sign in (1, -1)
    for dist in range(1, 5)
    if dist < 4 or sign == (1 if plane == 0 else -1)
]
SEM = {name: at for at, name in enumerate(GATHER + CORE + REDUCE + [("rx",)])}
SLOT = {name: at for at, name in enumerate(REDUCE)}


def split_bf16(value):
    high = value.astype(BF16)
    return high, (value - high.astype(F32)).astype(BF16)


def exchange(
    orb_hbm, ker_hbm, out_ref, ker, orb, gat, lhs, rhs, pair_rhs, dens, wts, part, landed, folded, ssem, rsem, lsem
):
    b = lax.axis_index("blk")
    s = lax.axis_index("split")
    xh, z, c = b // (NZ * NC), (b // NC) % NZ, b % NC
    xl, y = s // NY, s % NY

    def blk_of(plane, off):
        return ((xh + plane) % NX) * (NZ * NC) + ((z + off + NZ) % NZ) * NC + c

    x_peer = (blk_of(1, 0), s)
    core_peer = (b + 1 - 2 * c, s)
    z_peer = {sign: (blk_of(0, sign), s) for sign in (1, -1)}
    y_peer = {sign: (b, xl * NY + (y + sign + NY) % NY) for sign in (1, -1)}
    xl_peer = (b, ((xl + 1) % NXL) * NY + y)
    peers = [x_peer, core_peer, z_peer[1], z_peer[-1], y_peer[1], y_peer[-1], xl_peer]

    ker_copy = pltpu.make_async_copy(ker_hbm.at[:, 0, :], ker, lsem.at[0])
    orb_copy = pltpu.make_async_copy(orb_hbm, orb, lsem.at[1])

    def share_rows(block):
        return pl.ds(pl.multiple_of(block * SH, SH), SH)

    own_copy = pltpu.make_async_copy(orb_hbm.at[share_rows(s)], gat.at[share_rows(b)], lsem.at[2])
    own_copy.start()
    orb_copy.start()
    ker_copy.start()

    barrier = pltpu.get_barrier_semaphore()
    for peer in peers:
        pl.semaphore_signal(barrier, inc=1, device_id=peer, device_id_type=MESH)
    pl.semaphore_wait(barrier, len(peers))

    started = []

    def remote(name, src, dst, peer):
        return pltpu.make_async_remote_copy(
            src_ref=src,
            dst_ref=dst,
            send_sem=ssem.at[SEM[name]],
            recv_sem=rsem.at[SEM[name]],
            device_id=peer,
            device_id_type=MESH,
        )

    def send(name, src, dst, peer):
        copy = remote(name, src, dst, peer)
        copy.start()
        started.append(copy)

    def send_share(name, block, peer):
        rows = share_rows(block)
        send(name, gat.at[rows], gat.at[rows], peer)

    def wait_share(name, block, peer):
        rows = share_rows(block)
        remote(name, gat.at[rows], gat.at[rows], peer).wait_recv()

    def has_hop(plane, sign, hop):
        return ("gz", plane, sign, hop) in SEM

    own_copy.wait()
    send_share(("gx",), b, x_peer)
    send_share(("gz", 0, 1, 1), b, z_peer[1])
    send_share(("gz", 0, -1, 1), b, z_peer[-1])
    send_share(("gc", 0, 0), b, core_peer)
    other = blk_of(1, 0)
    wait_share(("gx",), other, x_peer)
    send_share(("gz", 1, 1, 1), other, z_peer[1])
    send_share(("gz", 1, -1, 1), other, z_peer[-1])
    send_share(("gc", 1, 0), other, core_peer)

    def gather_hop(hop):
        for plane in (0, 1):
            for sign in (1, -1):
                if not has_hop(plane, sign, hop):
                    continue
                off = -sign * hop
                block = blk_of(plane, off)
                wait_share(("gz", plane, sign, hop), block, z_peer[sign])
                if has_hop(plane, sign, hop + 1):
                    send_share(("gz", plane, sign, hop + 1), block, z_peer[sign])
                send_share(("gc", plane, off % NZ), block, core_peer)

    def wait_core(offs):
        for off in offs:
            for plane in (0, 1):
                block = blk_of(plane, off) + 1 - 2 * c
                wait_share(("gc", plane, off % NZ), block, core_peer)

    odd = z % 2
    half = NZ // 2
    pair0 = z // 2
    near = 2 * odd - 1
    pairs = [pair0, (pair0 + near + half) % half, (pair0 - near + half) % half, (pair0 + 2) % half]
    width = 2 * NC * SH

    def batch(pair, first):
        for plane in (0, 1):
            rows = pl.ds(pl.multiple_of(plane * (NZ * NC * SH) + pair * width, width), width)
            high, low = split_bf16(gat[rows, :])
            at = pl.ds(plane * width, width)
            rhs[at, pl.ds(0, NORB)] = high
            rhs[at, pl.ds(NORB, NORB)] = high
            rhs[at, pl.ds(2 * NORB, NORB)] = low
            pair_rhs[pl.ds(plane * width, width), :] = high
            pair_rhs[pl.ds((NX + plane) * width, width), :] = high
            pair_rhs[pl.ds((2 * NX + plane) * width, width), :] = low
        dens[...] = lax.dot_general(
            lhs[...], rhs[...], (((1,), (1,)), ((), ())), preferred_element_type=F32
        )
        for plane in (0, 1):
            cols = pl.ds(pl.multiple_of(plane * (NZ * NC * SH) + pair * width, width), width)
            weighted = dens[:, pl.ds(plane * width, width)] * ker[:, cols]
            high, low = split_bf16(weighted)
            wts[:, pl.ds(plane * width, width)] = high
            wts[:, pl.ds((NX + plane) * width, width)] = low
            wts[:, pl.ds((2 * NX + plane) * width, width)] = high
        product = jnp.dot(wts[...], pair_rhs[...], preferred_element_type=F32)
        if first:
            part[...] = product
        else:
            part[...] += product

    orb_copy.wait()
    high, low = split_bf16(orb[...])
    lhs[:, pl.ds(0, NORB)] = high
    lhs[:, pl.ds(NORB, NORB)] = low
    lhs[:, pl.ds(2 * NORB, NORB)] = high

    gather_hop(1)
    gather_hop(2)
    ker_copy.wait()
    wait_core([0, 1, -1])
    batch(pairs[0], True)
    gather_hop(3)
    wait_core([2, -2])
    batch(pairs[1], False)
    gather_hop(4)
    wait_core([3, -3])
    batch(pairs[2], False)
    wait_core([4])
    batch(pairs[3], False)

    def target_rows(plane, off):
        share = ((xl + plane) % NXL) * NY + (y + off + NY) % NY
        return share_rows(share)

    def slot_rows(name):
        return pl.ds(SLOT[name] * SH, SH)

    def send_partial(plane, sign, dist):
        name = ("r", plane, sign, dist)
        send(name, part.at[target_rows(plane, sign * dist)], landed.at[slot_rows(name)], y_peer[sign])

    def wait_partial(plane, sign, dist):
        name = ("r", plane, sign, dist)
        remote(name, part.at[slot_rows(name)], landed.at[slot_rows(name)], y_peer[sign]).wait_recv()
        return landed[slot_rows(name), :]

    chains = [(1, -1), (1, 1), (0, 1), (0, -1)]
    longest = {chain: max(n[3] for n in REDUCE if n[1:3] == chain) for chain in chains}
    for step in range(4):
        for plane, sign in chains:
            dist = longest[plane, sign] - step
            if dist < 1:
                continue
            if step:
                rows = target_rows(plane, sign * dist)
                part[rows, :] += wait_partial(plane, sign, dist + 1)
            send_partial(plane, sign, dist)

    folded[pl.ds(0, SH), :] = (
        part[target_rows(1, 0), :] + wait_partial(1, 1, 1) + wait_partial(1, -1, 1)
    )
    send(("rx",), folded.at[pl.ds(0, SH)], folded.at[pl.ds(SH, SH)], xl_peer)
    mine = part[target_rows(0, 0), :] + wait_partial(0, 1, 1) + wait_partial(0, -1, 1)
    remote(("rx",), folded.at[pl.ds(0, SH)], folded.at[pl.ds(SH, SH)], xl_peer).wait_recv()
    out_ref[...] = mine + folded[pl.ds(SH, SH), :]

    for copy in started:
        copy.wait_send()


def per_device(orbitals, kernel):
    columns = kernel.shape[2]
    return pl.pallas_call(
        exchange,
        out_shape=jax.ShapeDtypeStruct((SH, NORB), F32),
        in_specs=[pl.BlockSpec(memory_space=pltpu.HBM)] * 2,
        out_specs=pl.BlockSpec(memory_space=pltpu.VMEM),
        scratch_shapes=[
            pltpu.VMEM((PB, columns), F32),
            pltpu.VMEM((PB, NORB), F32),
            pltpu.VMEM((columns, NORB), F32),
            pltpu.VMEM((PB, 3 * NORB), BF16),
            pltpu.VMEM((256, 3 * NORB), BF16),
            pltpu.VMEM((3 * 256, NORB), BF16),
            pltpu.VMEM((PB, 256), F32),
            pltpu.VMEM((PB, 3 * 256), BF16),
            pltpu.VMEM((PB, NORB), F32),
            pltpu.VMEM((len(REDUCE) * SH, NORB), F32),
            pltpu.VMEM((2 * SH, NORB), F32),
            pltpu.SemaphoreType.DMA((len(SEM),)),
            pltpu.SemaphoreType.DMA((len(SEM),)),
            pltpu.SemaphoreType.DMA((3,)),
        ],
        compiler_params=pltpu.CompilerParams(
            collective_id=0, has_side_effects=True, vmem_limit_bytes=67_043_328
        ),
    )(orbitals, kernel)


def solution(mesh):
    placed = (P("blk", None), P("blk", "split", None))
    return jax.shard_map(
        per_device, mesh=mesh, in_specs=placed, out_specs=P(("blk", "split"), None), check_vma=False
    )
```

time: 320 us -> 55.8 us (0.17)
  the two profiles are of different devices: /device:TPU:4 before, /device:TPU:2 now
where the time goes in v1:
time: 55.8 us; the launch traced here: 55.6 us
  Pallas kernels  54.1 us (97%)
  local copies, waits for them, and re-layouts  1.47 us (3%)
    pallas_call x1, Pallas kernels, per_device(): pl.pallas_call(exchange, out_shape=jax.ShapeDtypeStruct((SH, NORB), F32),...  54.1 us
    unnamed x1, local copies, waits for them, and re-layouts  1.47 us

profile of v1, /device:TPU:2, one launch (start us, length us, event | category | flops | bytes accessed | tf_op | source)
XLA Modules:
  0.0 55.6 jit_solution(2470056292515247416)
XLA Ops:
  0.0 54.1 %shard_map.28 = f32[32,512]{1,0:T(8,128)} custom-call(f32[512,512]{1,0:T(8,128)} %orb_hbm.1, f32[512,1,1024]{2,1,0:T(1,128)} %ker_hbm.1), custom_call_target="tpu_custom_call" | custom-call | tf_op jit(solution)/shard_map/pallas_call | solution.py:231
  54.1 1.5 %copy.4 = f32[32,512]{1,0:T(8,128)} copy(f32[32,512]{1,0:T(8,128)} %shard_map.28) | data formatting | bytes 131072

commit v2 on v0

v2 whole, which is shorter than its diff:
```python
import jax
import jax.numpy as jnp
from jax import lax
from jax.experimental import pallas as pl
from jax.experimental.pallas import tpu as pltpu
from jax.sharding import PartitionSpec as P

MESH = pl.DeviceIdType.MESH
F32 = jnp.float32
BF16 = jnp.bfloat16

NX, NZ, NC = 2, 8, 2
NXL, NY = 2, 8
SH = 32
NORB = 512
PB = 512
GCH = 2
RCH = 2
GR = SH // GCH
RR = SH // RCH
WIDE = 2 * NC * SH
BATCH = 2 * WIDE


def longest(plane, sign):
    return 4 if sign == (1 if plane == 0 else -1) else 3


CHAINS = [(plane, sign) for plane in (0, 1) for sign in (1, -1)]
GATHER = [("gx", k) for k in range(GCH)] + [
    ("gz", plane, sign, hop, k)
    for plane, sign in CHAINS
    for hop in range(1, longest(plane, sign) + 1)
    for k in range(GCH)
]
NEAR, FAR = (0, 1, 7, 2, 6), (3, 5, 4)
CORE = [("gc", plane, off in NEAR) for plane in (0, 1) for off in (0, 4)]
REDUCE = [
    ("r", plane, sign, dist, k)
    for plane, sign in CHAINS
    for dist in range(1, longest(plane, sign) + 1)
    for k in range(RCH)
]
FOLD = [("rx", k) for k in range(RCH)]
SEM = {name: at for at, name in enumerate(GATHER + CORE + REDUCE + FOLD)}
SLOT = {name: at for at, name in enumerate(REDUCE)}
KINDS = {"gx": (0, SH), "gz": (1, len(GATHER) * GR - SH), "gc": (2, 2 * NZ * SH), "r": (3, len(REDUCE) * RR), "rx": (4, SH)}


def split_bf16(value):
    high = value.astype(BF16)
    return high, (value - high.astype(F32)).astype(BF16)


def rows_by_rows(a, b):
    return lax.dot_general(a, b, (((1,), (1,)), ((), ())), preferred_element_type=F32)


def rows_by_cols(a, b):
    return jnp.dot(a, b, preferred_element_type=F32)


def exchange(
    orb_hbm, ker_hbm, out_ref, ker, orb, gat, lhs, rhs, dens, wts, part, landed, folded, ssem, rsem, lsem
):
    b = lax.axis_index("blk")
    s = lax.axis_index("split")
    xh, z, c = b // (NZ * NC), (b // NC) % NZ, b % NC
    xl, y = s // NY, s % NY

    def blk_of(plane, off):
        return ((xh + plane) % NX) * (NZ * NC) + ((z + off + NZ) % NZ) * NC + c

    x_peer = (blk_of(1, 0), s)
    core_peer = (b + 1 - 2 * c, s)
    z_peer = {sign: (blk_of(0, sign), s) for sign in (1, -1)}
    y_peer = {sign: (b, xl * NY + (y + sign + NY) % NY) for sign in (1, -1)}
    xl_peer = (b, ((xl + 1) % NXL) * NY + y)
    peers = [x_peer, core_peer, z_peer[1], z_peer[-1], y_peer[1], y_peer[-1], xl_peer]

    barrier = pltpu.get_barrier_semaphore()
    for peer in peers:
        pl.semaphore_signal(barrier, inc=1, device_id=peer, device_id_type=MESH)

    def piece(block, k):
        return pl.ds(pl.multiple_of(block * SH + k * GR, 8), GR)

    orb_copy = pltpu.make_async_copy(orb_hbm, orb, lsem.at[0])
    ker_copy = pltpu.make_async_copy(ker_hbm.at[:, 0, :], ker, lsem.at[1])
    own_copy = pltpu.make_async_copy(
        orb_hbm.at[pl.ds(pl.multiple_of(s * SH, SH), SH)],
        gat.at[pl.ds(pl.multiple_of(b * SH, SH), SH)],
        lsem.at[2],
    )
    own_copy.start()
    orb_copy.start()
    ker_copy.start()

    pl.semaphore_wait(barrier, len(peers))

    def remote(name, src, dst, peer):
        return pltpu.make_async_remote_copy(
            src_ref=src,
            dst_ref=dst,
            send_sem=ssem.at[KINDS[name[0]][0]],
            recv_sem=rsem.at[SEM[name]],
            device_id=peer,
            device_id_type=MESH,
        )

    def send(name, src, dst, peer):
        remote(name, src, dst, peer).start()

    def send_own(name, k, peer):
        send(name, orb_hbm.at[piece(s, k)], gat.at[piece(b, k)], peer)

    def send_piece(name, block, k, peer):
        send(name, gat.at[piece(block, k)], gat.at[piece(block, k)], peer)

    def wait_piece(name, block, k, peer):
        remote(name, gat.at[piece(block, k)], gat.at[piece(block, k)], peer).wait_recv()

    for k in range(GCH):
        send_own(("gx", k), k, x_peer)
        for sign in (1, -1):
            send_own(("gz", 0, sign, 1, k), k, z_peer[sign])
    for k in range(GCH):
        send_own(("gc", 0, True), k, core_peer)

    orb_copy.wait()
    high, low = split_bf16(orb[...])
    lhs[:, pl.ds(0, NORB)] = high
    lhs[:, pl.ds(NORB, NORB)] = low

    def take_x(k):
        block = blk_of(1, 0)
        wait_piece(("gx", k), block, k, x_peer)
        for sign in (1, -1):
            send_piece(("gz", 1, sign, 1, k), block, k, z_peer[sign])
        send_piece(("gc", 1, True), block, k, core_peer)

    def take_hop(plane, hop, k):
        for sign in (1, -1):
            if hop > longest(plane, sign):
                continue
            block = blk_of(plane, -sign * hop)
            wait_piece(("gz", plane, sign, hop, k), block, k, z_peer[sign])
            if hop < longest(plane, sign):
                send_piece(("gz", plane, sign, hop + 1, k), block, k, z_peer[sign])
            send_piece(("gc", plane, hop <= 2), block, k, core_peer)

    def wait_core(plane, is_near):
        rows = pl.ds(0, len(NEAR if is_near else FAR) * SH)
        remote(("gc", plane, is_near), gat.at[rows], gat.at[rows], core_peer).wait_recv()

    half = NZ // 2
    pair0 = z // 2
    near = 2 * (z % 2) - 1
    pairs = {
        "near": [pair0, (pair0 + near + half) % half],
        "far": [(pair0 - near + half) % half, (pair0 + 2) % half],
    }

    def columns(plane, pair):
        at = ((xh + plane) % NX) * (NZ * NC * SH) + pair * WIDE
        return pl.ds(pl.multiple_of(at, WIDE), WIDE)

    def weigh(plane, which):
        for at, pair in enumerate(pairs[which]):
            high, low = split_bf16(gat[columns(plane, pair), :])
            rhs[pl.ds(at * WIDE, WIDE), pl.ds(0, NORB)] = high
            rhs[pl.ds(at * WIDE, WIDE), pl.ds(NORB, NORB)] = low
        g_high, g_low = rhs[:, pl.ds(0, NORB)], rhs[:, pl.ds(NORB, NORB)]
        for start in (0, PB // 2):
            rows = pl.ds(start, PB // 2)
            o_high, o_low = lhs[rows, pl.ds(0, NORB)], lhs[rows, pl.ds(NORB, NORB)]
            dens[rows, :] = (
                rows_by_rows(o_high, g_high) + rows_by_rows(o_low, g_high) + rows_by_rows(o_high, g_low)
            )
        for at, pair in enumerate(pairs[which]):
            weighted = dens[:, pl.ds(at * WIDE, WIDE)] * ker[:, columns(plane, pair)]
            high, low = split_bf16(weighted)
            wts[:, pl.ds(at * WIDE, WIDE)] = high
            wts[:, pl.ds(BATCH + at * WIDE, WIDE)] = low

    def apply(first):
        w_high, w_low = wts[:, pl.ds(0, BATCH)], wts[:, pl.ds(BATCH, BATCH)]
        for start in (0, NORB // 2):
            cols = pl.ds(start, NORB // 2)
            g_high, g_low = rhs[:, cols], rhs[:, pl.ds(NORB + start, NORB // 2)]
            product = (
                rows_by_cols(w_high, g_high) + rows_by_cols(w_low, g_high) + rows_by_cols(w_high, g_low)
            )
            part[:, cols] = product if first else part[:, cols] + product

    steps = []
    for k in range(GCH):
        steps.append((3.8 + 1.4 * k, lambda k=k: take_x(k)))
        for hop in range(1, 5):
            steps.append((2.4 * hop + 0.7 * k, lambda hop=hop, k=k: take_hop(0, hop, k)))
            steps.append((4.2 + 2.4 * hop + 0.7 * k, lambda hop=hop, k=k: take_hop(1, hop, k)))

    def near_own():
        ker_copy.wait()
        own_copy.wait()
        wait_core(0, True)
        weigh(0, "near")

    def near_other():
        wait_core(1, True)
        weigh(1, "near")

    def far_own():
        wait_core(0, False)
        weigh(0, "far")

    steps.append((6.3, near_own))
    steps.append((7.6, lambda: apply(True)))
    steps.append((10.6, near_other))
    steps.append((11.4, lambda: apply(False)))
    steps.append((12.2, far_own))
    steps.append((12.3, lambda: apply(False)))
    for _, step in sorted(steps, key=lambda entry: entry[0]):
        step()
    wait_core(1, False)
    weigh(1, "far")
    apply(False)

    def target(plane, off, k):
        share = ((xl + plane) % NXL) * NY + (y + off + NY) % NY
        return pl.ds(pl.multiple_of(share * SH + k * RR, 8), RR)

    def slot(name):
        return pl.ds(SLOT[name] * RR, RR)

    def send_partial(plane, sign, dist, k):
        name = ("r", plane, sign, dist, k)
        send(name, part.at[target(plane, sign * dist, k)], landed.at[slot(name)], y_peer[sign])

    def take_partial(plane, sign, dist, k):
        name = ("r", plane, sign, dist, k)
        remote(name, landed.at[slot(name)], landed.at[slot(name)], y_peer[sign]).wait_recv()
        return landed[slot(name), :]

    order = [(1, -1), (1, 1), (0, 1), (0, -1)]
    for step in range(4):
        for k in range(RCH):
            for plane, sign in order:
                dist = longest(plane, sign) - step
                if dist < 1:
                    continue
                if step:
                    part[target(plane, sign * dist, k), :] += take_partial(plane, sign, dist + 1, k)
                send_partial(plane, sign, dist, k)

    for k in range(RCH):
        here, there = pl.ds(k * RR, RR), pl.ds(SH + k * RR, RR)
        folded[here, :] = (
            part[target(1, 0, k), :] + take_partial(1, 1, 1, k) + take_partial(1, -1, 1, k)
        )
        send(("rx", k), folded.at[here], folded.at[there], xl_peer)
    for k in range(RCH):
        here, there = pl.ds(k * RR, RR), pl.ds(SH + k * RR, RR)
        mine = part[target(0, 0, k), :] + take_partial(0, 1, 1, k) + take_partial(0, -1, 1, k)
        remote(("rx", k), folded.at[here], folded.at[there], xl_peer).wait_recv()
        out_ref[here, :] = mine + folded[there, :]

    for name, peer in (("gx", 0), x_peer), (("gz", 0, 1, 1, 0), z_peer[1]), (("gc", 0, True), core_peer):
        rows = pl.ds(0, KINDS[name[0]][1])
        remote(name, gat.at[rows], gat.at[rows], peer).wait_send()
    rows = pl.ds(0, KINDS["r"][1])
    remote(("r", 0, 1, 1, 0), landed.at[rows], landed.at[rows], y_peer[1]).wait_send()
    rows = pl.ds(0, SH)
    remote(("rx", 0), folded.at[rows], folded.at[rows], xl_peer).wait_send()


def per_device(orbitals, kernel):
    columns = kernel.shape[2]
    return pl.pallas_call(
        exchange,
        out_shape=jax.ShapeDtypeStruct((SH, NORB), F32),
        in_specs=[pl.BlockSpec(memory_space=pltpu.HBM)] * 2,
        out_specs=pl.BlockSpec(memory_space=pltpu.VMEM),
        scratch_shapes=[
            pltpu.VMEM((PB, columns), F32),
            pltpu.VMEM((PB, NORB), F32),
            pltpu.VMEM((columns, NORB), F32),
            pltpu.VMEM((PB, 2 * NORB), BF16),
            pltpu.VMEM((BATCH, 2 * NORB), BF16),
            pltpu.VMEM((PB, BATCH), F32),
            pltpu.VMEM((PB, 2 * BATCH), BF16),
            pltpu.VMEM((PB, NORB), F32),
            pltpu.VMEM((len(REDUCE) * RR, NORB), F32),
            pltpu.VMEM((2 * SH, NORB), F32),
            pltpu.SemaphoreType.DMA((len(KINDS),)),
            pltpu.SemaphoreType.DMA((len(SEM),)),
            pltpu.SemaphoreType.DMA((3,)),
        ],
        compiler_params=pltpu.CompilerParams(
            collective_id=0, has_side_effects=True, vmem_limit_bytes=50_000_000
        ),
    )(*(pltpu.with_memory_space_constraint(array, pltpu.HBM) for array in (orbitals, kernel)))


def solution(mesh):
    placed = (P("blk", None), P("blk", "split", None))
    return jax.shard_map(
        per_device, mesh=mesh, in_specs=placed, out_specs=P(("blk", "split"), None), check_vma=False
    )
```

time: 320 us -> 53 us (0.17)
  the two profiles are of different devices: /device:TPU:4 before, /device:TPU:1 now
where the time goes in v2:
time: 53 us; the launch traced here: 52.7 us
  Pallas kernels  52 us (98%)
  local copies, waits for them, and re-layouts  0.63 us (1%)
    pallas_call x1, Pallas kernels, per_device(): pl.pallas_call(exchange, out_shape=jax.ShapeDtypeStruct((SH, NORB), F32),...  52 us

profile of v2, /device:TPU:1, one launch (start us, length us, event | category | flops | bytes accessed | tf_op | source)
XLA Modules:
  0.0 52.7 jit_solution(520804976806740165)
XLA Ops:
  0.0 52.0 %shard_map.28 = f32[32,512]{1,0:T(8,128)S(1)} custom-call(f32[512,512]{1,0:T(8,128)} %orb_hbm.1, f32[512,1,1024]{2,1,0:T(1,128)} %ker_hbm.1), custom_call_target="tpu_custom_call" | custom-call | tf_op jit(solution)/shard_map/pallas_call | solution.py:279
  52.0 0.6 %copy.4 = f32[32,512]{1,0:T(8,128)} copy(f32[32,512]{1,0:T(8,128)S(1)} %shard_map.28) | data formatting | bytes 131072

commit v3 on v2

v3 whole, which is shorter than its diff:
```python
import jax
import jax.numpy as jnp
from jax import lax
from jax.experimental import pallas as pl
from jax.experimental.pallas import tpu as pltpu
from jax.sharding import PartitionSpec as P

MESH = pl.DeviceIdType.MESH
F32 = jnp.float32
BF16 = jnp.bfloat16

NX, NZ, NC = 2, 8, 2
NXL, NY = 2, 8
SH = 32
NORB = 512
PB = 512
GCH = 2
RCH = 2
GR = SH // GCH
RR = SH // RCH
WIDE = 2 * NC * SH
BATCH = 2 * WIDE


HOPS = 4


def longest(plane, sign):
    return 4 if sign == (1 if plane == 0 else -1) else 3


CHAINS = [(plane, sign) for plane in (0, 1) for sign in (1, -1)]


def group_of(plane, hop):
    return ("a" if hop < HOPS else "b") if plane == 0 else ("b" if hop < 2 else "c")


GATHER = [("gx", k) for k in range(GCH)] + [
    ("gz", plane, hop, k) for plane in (0, 1) for hop in range(1, HOPS + 1) for k in range(GCH)
]
CORE = [("gc", name) for name in "abc"]
IN_GROUP = {
    name: sum(group_of(plane, hop) == name for plane in (0, 1) for hop in range(HOPS + 1)) for name in "abc"
}
REDUCE = [
    ("r", plane, sign, dist, k)
    for plane, sign in CHAINS
    for dist in range(1, longest(plane, sign) + 1)
    for k in range(RCH)
]
FOLD = [("rx", k) for k in range(RCH)]
BACK = [(plane, hop) for plane in (0, 1) for hop in (1, 2, 3)]
MERGE = {"ma": [(0, 1), (0, 2)], "mb": [(0, 3)], "mc": [(1, 1), (1, 2), (1, 3)]}
RETURN = [("ret", plane) for plane in (0, 1)]
SEM = {name: at for at, name in enumerate(GATHER + CORE + REDUCE + FOLD + [(name,) for name in MERGE] + RETURN)}
SLOT = {name: at for at, name in enumerate(REDUCE)}
KINDS = {
    "gx": (0, SH), "gz": (1, 2 * HOPS * SH), "gc": (2, 2 * (HOPS + 1) * SH), "r": (3, len(REDUCE) * RR), "rx": (4, SH),
    "ma": (5, 2 * SH), "mb": (6, SH), "mc": (7, 3 * SH), "ret": (8, len(BACK) * SH),
}


def split_bf16(value):
    high = value.astype(BF16)
    return high, (value - high.astype(F32)).astype(BF16)


def rows_by_rows(a, b):
    return lax.dot_general(a, b, (((1,), (1,)), ((), ())), preferred_element_type=F32)


def rows_by_cols(a, b):
    return jnp.dot(a, b, preferred_element_type=F32)


def exchange(
    orb_hbm, ker_hbm, out_ref,
    ker, orb, gat, lhs, rhs, dens, wts, turned, part, landed, folded, back, merged, returned, ssem, rsem, lsem
):
    b = lax.axis_index("blk")
    s = lax.axis_index("split")
    xh, z, c = b // (NZ * NC), (b // NC) % NZ, b % NC
    xl, y = s // NY, s % NY

    def blk_of(plane, off):
        return ((xh + plane) % NX) * (NZ * NC) + ((z + off + NZ) % NZ) * NC + c

    def source(plane, hop):
        return blk_of(plane, -hop if plane == 0 else hop)

    x_peer = (blk_of(1, 0), s)
    core_peer = (b + 1 - 2 * c, s)
    z_peer = [(blk_of(0, 1), s), (blk_of(0, -1), s)]
    y_peer = {sign: (b, xl * NY + (y + sign + NY) % NY) for sign in (1, -1)}
    xl_peer = (b, ((xl + 1) % NXL) * NY + y)
    peers = [x_peer, core_peer, y_peer[1], y_peer[-1], xl_peer]
    peers += [(blk_of(plane, off), s) for plane in (0, 1) for off in (1, -1, 2, -2, 3, -3)]

    barrier = pltpu.get_barrier_semaphore()
    for peer in peers:
        pl.semaphore_signal(barrier, inc=1, device_id=peer, device_id_type=MESH)

    def piece(block, k):
        return pl.ds(pl.multiple_of(block * SH + k * GR, 8), GR)

    def share(block):
        return pl.ds(pl.multiple_of(block * SH, SH), SH)

    orb_copy = pltpu.make_async_copy(orb_hbm, orb, lsem.at[0])
    ker_copy = pltpu.make_async_copy(ker_hbm.at[:, 0, :], ker, lsem.at[1])
    own_copy = pltpu.make_async_copy(orb_hbm.at[share(s)], gat.at[share(b)], lsem.at[2])
    own_copy.start()
    orb_copy.start()
    ker_copy.start()

    half = NZ // 2
    pair0 = z // 2

    def columns(plane, off):
        pair = (pair0 + off + half) % half
        at = ((xh + plane) % NX) * (NZ * NC * SH) + pair * WIDE
        return pl.ds(pl.multiple_of(at, WIDE), WIDE)

    for plane, off in ((0, 1), (1, 5)):
        chip = ((xh + plane) % NX) * NZ + (z + off + 2 * (z % 2)) % NZ
        gat[pl.ds(pl.multiple_of(chip * NC * SH, NC * SH), NC * SH), :] = jnp.zeros((NC * SH, NORB), F32)

    pl.semaphore_wait(barrier, len(peers))

    def remote(name, src, dst, peer):
        return pltpu.make_async_remote_copy(
            src_ref=src,
            dst_ref=dst,
            send_sem=ssem.at[KINDS[name[0]][0]],
            recv_sem=rsem.at[SEM[name]],
            device_id=peer,
            device_id_type=MESH,
        )

    def send(name, src, dst, peer):
        remote(name, src, dst, peer).start()

    def send_own(name, k, peer):
        send(name, orb_hbm.at[piece(s, k)], gat.at[piece(b, k)], peer)

    def send_piece(name, block, k, peer):
        send(name, gat.at[piece(block, k)], gat.at[piece(block, k)], peer)

    def wait_piece(name, block, k, peer):
        remote(name, gat.at[piece(block, k)], gat.at[piece(block, k)], peer).wait_recv()

    for k in range(GCH):
        send_own(("gx", k), k, x_peer)
        send_own(("gz", 0, 1, k), k, z_peer[0])
    for k in range(GCH):
        send_own(("gc", group_of(0, 0)), k, core_peer)

    orb_copy.wait()
    high, low = split_bf16(orb[...])
    lhs[:, pl.ds(0, NORB)] = high
    lhs[:, pl.ds(NORB, NORB)] = low

    def take_x(k):
        block = source(1, 0)
        wait_piece(("gx", k), block, k, x_peer)
        send_piece(("gz", 1, 1, k), block, k, z_peer[1])
        send_piece(("gc", group_of(1, 0)), block, k, core_peer)

    def take_hop(plane, hop, k):
        block = source(plane, hop)
        wait_piece(("gz", plane, hop, k), block, k, z_peer[plane])
        if hop < HOPS:
            send_piece(("gz", plane, hop + 1, k), block, k, z_peer[plane])
        send_piece(("gc", group_of(plane, hop)), block, k, core_peer)

    def wait_core(name):
        rows = pl.ds(0, IN_GROUP[name] * SH)
        remote(("gc", name), gat.at[rows], gat.at[rows], core_peer).wait_recv()

    batches = {
        "a": [columns(0, 0), columns(0, -1)],
        "b": [columns(0, -2), columns(1, 0)],
        "c": [columns(1, 1), columns(1, 2)],
    }

    def weigh(name):
        wait_core(name)
        for at, rows in enumerate(batches[name]):
            high, low = split_bf16(gat[rows, :])
            rhs[pl.ds(at * WIDE, WIDE), pl.ds(0, NORB)] = high
            rhs[pl.ds(at * WIDE, WIDE), pl.ds(NORB, NORB)] = low
        g_high, g_low = rhs[:, pl.ds(0, NORB)], rhs[:, pl.ds(NORB, NORB)]
        for start in (0, PB // 2):
            rows = pl.ds(start, PB // 2)
            o_high, o_low = lhs[rows, pl.ds(0, NORB)], lhs[rows, pl.ds(NORB, NORB)]
            dens[rows, :] = (
                rows_by_rows(o_high, g_high) + rows_by_rows(o_low, g_high) + rows_by_rows(o_high, g_low)
            )
        for at, cols in enumerate(batches[name]):
            high, low = split_bf16(dens[:, pl.ds(at * WIDE, WIDE)] * ker[:, cols])
            wts[:, pl.ds(at * WIDE, WIDE)] = high
            wts[:, pl.ds(BATCH + at * WIDE, WIDE)] = low

    def apply(first):
        w_high, w_low = wts[:, pl.ds(0, BATCH)], wts[:, pl.ds(BATCH, BATCH)]
        for start in (0, NORB // 2):
            cols = pl.ds(start, NORB // 2)
            g_high, g_low = rhs[:, cols], rhs[:, pl.ds(NORB + start, NORB // 2)]
            product = (
                rows_by_cols(w_high, g_high) + rows_by_cols(w_low, g_high) + rows_by_cols(w_high, g_low)
            )
            part[:, cols] = product if first else part[:, cols] + product

    def apply_back(name):
        for start in (0, PB // 2):
            rows = pl.ds(start, PB // 2)
            turned[:, pl.ds(start, PB // 2)] = wts[rows, pl.ds(0, BATCH)].T
            turned[:, pl.ds(PB + start, PB // 2)] = wts[rows, pl.ds(BATCH, BATCH)].T
        w_high, w_low = turned[:, pl.ds(0, PB)], turned[:, pl.ds(PB, PB)]
        for start in (0, NORB // 2):
            cols = pl.ds(start, NORB // 2)
            o_high, o_low = lhs[:, cols], lhs[:, pl.ds(NORB + start, NORB // 2)]
            product = (
                rows_by_cols(w_high, o_high) + rows_by_cols(w_low, o_high) + rows_by_cols(w_high, o_low)
            )
            for at, rows in enumerate(batches[name]):
                back[rows, cols] = product[at * WIDE : (at + 1) * WIDE, :]

    def merge_rows(plane, hop):
        return pl.ds(BACK.index((plane, hop)) * SH, SH)

    def send_merge(name):
        for plane, hop in MERGE[name]:
            block = source(plane, hop) + 1 - 2 * c
            send((name,), back.at[share(block)], merged.at[merge_rows(plane, hop)], core_peer)

    def merge(name):
        rows = pl.ds(0, len(MERGE[name]) * SH)
        remote((name,), back.at[rows], merged.at[rows], core_peer).wait_recv()
        for plane, hop in MERGE[name]:
            back[share(source(plane, hop)), :] += merged[merge_rows(plane, hop), :]

    def send_back(plane):
        for hop in (3, 2, 1):
            block = source(plane, hop)
            send(("ret", plane), back.at[share(block)], returned.at[merge_rows(plane, hop)], (block, s))

    steps = []
    for k in range(GCH):
        steps.append((3.8 + 1.0 * k, lambda k=k: take_x(k)))
        for hop in range(1, HOPS + 1):
            steps.append((2.5 * hop + 0.5 * k, lambda hop=hop, k=k: take_hop(0, hop, k)))
            steps.append((4.3 + 2.5 * hop + 0.5 * k, lambda hop=hop, k=k: take_hop(1, hop, k)))

    def first_weigh():
        ker_copy.wait()
        own_copy.wait()
        weigh("a")

    steps.append((10.61, first_weigh))
    steps.append((10.62, lambda: apply(True)))
    steps.append((11.9, lambda: apply_back("a")))
    steps.append((11.91, lambda: send_merge("ma")))
    steps.append((12.41, lambda: weigh("b")))
    steps.append((12.42, lambda: apply(False)))
    steps.append((12.43, lambda: apply_back("b")))
    steps.append((12.44, lambda: send_merge("mb")))
    for _, step in sorted(steps, key=lambda entry: entry[0]):
        step()
    weigh("c")
    apply(False)

    def target(plane, off, k):
        at = ((xl + plane) % NXL) * NY + (y + off + NY) % NY
        return pl.ds(pl.multiple_of(at * SH + k * RR, 8), RR)

    def slot(name):
        return pl.ds(SLOT[name] * RR, RR)

    def send_partial(plane, sign, dist, k):
        name = ("r", plane, sign, dist, k)
        send(name, part.at[target(plane, sign * dist, k)], landed.at[slot(name)], y_peer[sign])

    def take_partial(plane, sign, dist, k):
        name = ("r", plane, sign, dist, k)
        remote(name, landed.at[slot(name)], landed.at[slot(name)], y_peer[sign]).wait_recv()
        return landed[slot(name), :]

    def reduce_step(step):
        for k in range(RCH):
            for plane, sign in ((1, -1), (1, 1), (0, 1), (0, -1)):
                dist = longest(plane, sign) - step
                if dist < 1:
                    continue
                if step:
                    part[target(plane, sign * dist, k), :] += take_partial(plane, sign, dist + 1, k)
                send_partial(plane, sign, dist, k)

    reduce_step(0)
    apply_back("c")
    send_merge("mc")
    merge("ma")
    merge("mb")
    send_back(0)
    reduce_step(1)
    merge("mc")
    send_back(1)
    reduce_step(2)
    reduce_step(3)

    for k in range(RCH):
        here, there = pl.ds(k * RR, RR), pl.ds(SH + k * RR, RR)
        folded[here, :] = (
            part[target(1, 0, k), :] + take_partial(1, 1, 1, k) + take_partial(1, -1, 1, k)
        )
        send(("rx", k), folded.at[here], folded.at[there], xl_peer)
    for plane in (0, 1):
        rows = pl.ds(plane * 3 * SH, 3 * SH)
        remote(("ret", plane), returned.at[rows], returned.at[rows], z_peer[0]).wait_recv()
    for k in range(RCH):
        here, there = pl.ds(k * RR, RR), pl.ds(SH + k * RR, RR)
        mine = part[target(0, 0, k), :] + take_partial(0, 1, 1, k) + take_partial(0, -1, 1, k)
        for at in range(len(BACK)):
            mine += returned[pl.ds(at * SH + k * RR, RR), :]
        remote(("rx", k), folded.at[here], folded.at[there], xl_peer).wait_recv()
        out_ref[here, :] = mine + folded[there, :]

    for name, buffer in (
        (("gx", 0), gat), (("gz", 0, 1, 0), gat), (("gc", "a"), gat), (("r", 0, 1, 1, 0), landed), (("rx", 0), folded),
        (("ma",), back), (("mb",), back), (("mc",), back), (("ret", 0), back),
    ):
        rows = pl.ds(0, KINDS[name[0]][1])
        remote(name, buffer.at[rows], buffer.at[rows], core_peer).wait_send()


def per_device(orbitals, kernel):
    columns = kernel.shape[2]
    return pl.pallas_call(
        exchange,
        out_shape=jax.ShapeDtypeStruct((SH, NORB), F32),
        in_specs=[pl.BlockSpec(memory_space=pltpu.HBM)] * 2,
        out_specs=pl.BlockSpec(memory_space=pltpu.VMEM),
        scratch_shapes=[
            pltpu.VMEM((PB, columns), F32),
            pltpu.VMEM((PB, NORB), F32),
            pltpu.VMEM((columns, NORB), F32),
            pltpu.VMEM((PB, 2 * NORB), BF16),
            pltpu.VMEM((BATCH, 2 * NORB), BF16),
            pltpu.VMEM((PB, BATCH), F32),
            pltpu.VMEM((PB, 2 * BATCH), BF16),
            pltpu.VMEM((BATCH, 2 * PB), BF16),
            pltpu.VMEM((PB, NORB), F32),
            pltpu.VMEM((len(REDUCE) * RR, NORB), F32),
            pltpu.VMEM((2 * SH, NORB), F32),
            pltpu.VMEM((columns, NORB), F32),
            pltpu.VMEM((len(BACK) * SH, NORB), F32),
            pltpu.VMEM((len(BACK) * SH, NORB), F32),
            pltpu.SemaphoreType.DMA((len(KINDS),)),
            pltpu.SemaphoreType.DMA((len(SEM),)),
            pltpu.SemaphoreType.DMA((3,)),
        ],
        compiler_params=pltpu.CompilerParams(
            collective_id=0, has_side_effects=True, vmem_limit_bytes=50_000_000
        ),
    )(*(pltpu.with_memory_space_constraint(array, pltpu.HBM) for array in (orbitals, kernel)))


def solution(mesh):
    placed = (P("blk", None), P("blk", "split", None))
    return jax.shard_map(
        per_device, mesh=mesh, in_specs=placed, out_specs=P(("blk", "split"), None), check_vma=False
    )
```

time: 53 us -> 53.7 us (1.013)
  Pallas kernels: 52 us -> 53 us
    pallas_call x1, Pallas kernels: 52 us -> 53 us  [per_device(): pl.pallas_call(exchange, out_shape=jax.ShapeDtypeStruct((SH, NORB), F32),...]
where the time goes in v3:
time: 53.7 us; the launch traced here: 53.6 us
  Pallas kernels  53 us (99%)
  local copies, waits for them, and re-layouts  0.63 us (1%)
    pallas_call x1, Pallas kernels, per_device(): pl.pallas_call(exchange, out_shape=jax.ShapeDtypeStruct((SH, NORB), F32),...  53 us

profile of v3, /device:TPU:1, one launch (start us, length us, event | category | flops | bytes accessed | tf_op | source)
XLA Modules:
  0.0 53.6 jit_solution(8224830372387363903)
XLA Ops:
  0.0 53.0 %shard_map.28 = f32[32,512]{1,0:T(8,128)S(1)} custom-call(f32[512,512]{1,0:T(8,128)} %orb_hbm.1, f32[512,1,1024]{2,1,0:T(1,128)} %ker_hbm.1), custom_call_target="tpu_custom_call" | custom-call | tf_op jit(solution)/shard_map/pallas_call | solution.py:339
  53.0 0.6 %copy.4 = f32[32,512]{1,0:T(8,128)} copy(f32[32,512]{1,0:T(8,128)S(1)} %shard_map.28) | data formatting | bytes 131072
